TPU v7x, 256 devices: a whole 4x4x8 slice. The times are simulated.
256 devices in a mesh: pole: 8 (over x, y_lo), sub: 32 (over y_hi, z, core).
Axes of the slice: x: 4, y: 4 (y_hi: 2, y_lo: 2; y = y_hi * 2 + y_lo), z: 8, core: 2. Of those that a mesh axis runs over, the one named last changes fastest.
Arguments:
- start_block: float32 [131072, 128], P('sub'), may hold values from -400 to 400
- inverses: float32 [8, 256, 512, 512], P('pole', 'sub'), may hold values from -1 to 3
- iface_rows: int32 [256, 2, 128], P('sub'), may hold values from 0 to 511, as said below
- neighbors: int32 [256, 2], P('sub'), may hold values from 0 to 255, as said below
- couplings: float32 [256, 2, 128], P('sub'), may hold values from 0.25 to 1
- pole_weights: float32 [8], P('pole'), may hold values from 0.25 to 1
Outputs:
- ortho_basis: float32 [131072, 128], P(('sub', 'pole'))
Inputs may be any that keep to these rules, and one draw needn't show every extreme that they name: `iface_rows`: in each subdomain the 256 listed rows are distinct. Subdomain j lies on index j // 8 of sub. neighbors[j, 0] lies on the previous index and neighbors[j, 1] on the next one, cyclically; over the subdomains of one index, the values in column 0 are the previous index's 8 subdomains, each once, and those in column 1 the next index's, each once.
All inputs are finite; a program needn't handle non-finite values.
Results may differ from a plain program's by a relative error of at most 0.0002.
Values sent between devices are 32-bit elements; how exact they have to be, the bound alone decides.
A program may use at most 64 MiB of HBM per device.

v0:
```python
import math
import jax
import jax.numpy as jnp
from jax import lax
from jax.sharding import PartitionSpec as P

precise = lax.Precision.HIGHEST


def extended_2(cells, sides, width):
    for axis, dim in sides:
        count = lax.axis_size(axis)
        head = lax.slice_in_dim(cells, 0, width, axis=dim)
        tail = lax.slice_in_dim(cells, cells.shape[dim] - width, cells.shape[dim], axis=dim)
        cells = jnp.concatenate(
            [
                lax.ppermute(tail, axis, [(i, (i + 1) % count) for i in range(count)]),
                cells,
                lax.ppermute(head, axis, [((i + 1) % count, i) for i in range(count)]),
            ],
            axis=dim,
        )
    return cells


def apply_blocks(blocks, fields):
    return jnp.einsum(
        "sij,sjv->siv", blocks, fields, precision=precise, preferred_element_type=jnp.float32
    )


def add_coupled(fields, iface_rows, neighbor_vals, couplings):

    def one_sub(field_one, rows_one, terms_one):
        field_one = field_one.at[rows_one[0]].add(terms_one[0])
        return field_one.at[rows_one[1]].add(terms_one[1])

    return jax.vmap(one_sub)(fields, iface_rows, couplings[..., None] * neighbor_vals)


def per_device(start_block, inverses, iface_rows, neighbors, couplings, pole_weights):
    blocks = inverses[0]
    sub_count = blocks.shape[0]
    block_len = blocks.shape[1]
    vec_count = start_block.shape[1]
    iface_len = iface_rows.shape[2]
    fields = start_block.reshape(sub_count, block_len, vec_count)
    first_pass = apply_blocks(blocks, fields)
    offsets = (jnp.arange(sub_count, dtype=jnp.int32) * block_len)[:, None, None]
    flat_index = (iface_rows + offsets).transpose(1, 0, 2).reshape(-1)
    outgoing = jnp.take(first_pass.reshape(sub_count * block_len, vec_count), flat_index, axis=0)
    half_rows = sub_count * iface_len
    extended = extended_2(outgoing, (("sub", 0),), half_rows)
    from_prev = extended[:half_rows].reshape(sub_count, iface_len, vec_count)
    from_next = extended[3 * half_rows :].reshape(sub_count, iface_len, vec_count)
    columns = jnp.arange(sub_count, dtype=jnp.int32)[None, :]
    choose_prev = (neighbors[:, 0:1] % sub_count == columns).astype(jnp.float32)
    choose_next = (neighbors[:, 1:2] % sub_count == columns).astype(jnp.float32)
    low_terms = jnp.einsum(
        "jk,kiv->jiv", choose_prev, from_prev, precision=precise, preferred_element_type=jnp.float32
    )
    high_terms = jnp.einsum(
        "jk,kiv->jiv", choose_next, from_next, precision=precise, preferred_element_type=jnp.float32
    )
    corrected = add_coupled(fields, iface_rows, jnp.stack([low_terms, high_terms], 1), couplings)
    weight = pole_weights[0]
    own_rows = sub_count * block_len // lax.axis_size("pole")
    pole_term = weight * apply_blocks(blocks, corrected).reshape(sub_count * block_len, vec_count)
    summed_poles = lax.psum(pole_term, "pole")
    filtered = lax.dynamic_slice_in_dim(
        summed_poles, lax.axis_index("pole") * own_rows, own_rows, 0
    )
    local_gram = jnp.dot(
        filtered.T, filtered, precision=precise, preferred_element_type=jnp.float32
    )
    gram_matrix = lax.psum(local_gram, ("pole", "sub"))
    lower_factor = jnp.linalg.cholesky(gram_matrix)
    total_rows = sub_count * block_len * lax.axis_size("sub")
    solved = lax.linalg.triangular_solve(
        lower_factor, filtered, left_side=False, lower=True, transpose_a=True
    )
    return math.sqrt(total_rows) * solved


def solution(mesh):
    placed = (
        P("sub", None),
        P("pole", "sub", None, None),
        P("sub", None, None),
        P("sub", None),
        P("sub", None, None),
        P("pole"),
    )
    return jax.shard_map(
        per_device, mesh=mesh, in_specs=placed, out_specs=P(("sub", "pole"), None), check_vma=False
    )
```

profile of v0, /device:TPU:1, one launch (start us, length us, event | category | flops | bytes accessed | tf_op | source)
XLA Modules:
  0.0 464.7 jit_solution(7205133361967697777)
XLA Ops:
  6.5 0.0 copy-start
  6.5 0.0 all-reduce.3.cloned.1.call-start
  6.5 1.6 copy.37
  8.1 0.0 copy-done
  8.1 0.1 compare_and_fusion
  8.3 10.6 %fusion.2 = f32[8,512,128]{2,1,0:T(8,128)} fusion(f32[8,512,128]{2,1,0:T(8,128)S(1)} %bitcast.62, f32[1,8,512,512]{3,2,1,0:T(8,128)} %param.7), kind=kOutput, calls=%fused_computation.5 | convolution fusion | flops 3221225472 | bytes 12582912 | tf_op jit(solution)/shard_map/sij,sjv->siv/dot_general | solution.py:27
  18.8 7.0 %gather_fusion = f32[2048,128]{1,0:T(8,128)S(1)} fusion(f32[4096,128]{1,0:T(8,128)} %bitcast.64, s32[2048]{0:T(1024)S(1)} %broadcast_clamp_fusion), kind=kCustom, calls=%fused_computation | custom fusion | bytes 2105344 | tf_op jit(solution)/shard_map/jit(_take)/gather | solution.py:51
  25.9 0.0 slice-start
  25.9 0.0 copy-start.2
  25.9 0.0 copy-start.3
  25.9 0.0 copy-start.1
  25.9 0.0 copy-start.4
  25.9 0.3 broadcast_select_fusion
  26.3 1.1 fusion.27
  27.3 3.2 collective-permute-start.1
  30.5 0.0 collective-permute-start
  30.6 0.0 slice-done
  30.6 0.0 copy-done.2
  30.6 0.0 copy-done.3
  30.6 0.1 multiply_reduce_fusion
  30.7 0.0 copy-done.1
  30.7 0.1 copy.12
  31.5 0.0 copy-done.4
  31.5 0.1 and_reduce_fusion
  31.6 5.8 %collective-permute-done.1 = f32[1024,128]{1,0:T(8,128)S(1)} collective-permute-done((f32[1024,128]{1,0:T(8,128)}, f32[1024,128]{1,0:T(8,128)S(1)}, u32[]{:S(2)}, u32[]{:S(2)}) %collective-permute-start.1) | collective-permute-done | bytes 524320 | tf_op jit(solution)/shard_map/ppermute | solution.py:19
  37.4 0.7 convolution_bitcast_fusion
  38.1 0.3 collective-permute-done
  38.4 0.7 convolution_bitcast_fusion.1
  39.0 0.3 maximum_multiply_fusion
  39.4 0.1 fusion.26
  39.5 0.1 copy.16
  39.6 0.1 copy.18
  39.7 6.8 %scatter_fusion = f32[4096,128]{1,0:T(8,128)S(1)} fusion(f32[4096,128]{1,0:T(8,128)S(1)} %copy.37, s32[1024]{0:T(1024)S(1)} %get-tuple-element.18, f32[1024,128]{1,0:T(8,128)S(1)} %bitcast.67), kind=kCustom, calls=%fused_computation.1 | custom fusion | flops 131072 | bytes 1576960
  46.5 7.0 %scatter_fusion.1 = f32[4096,128]{1,0:T(8,128)S(1)} fusion(f32[4096,128]{1,0:T(8,128)S(1)} %scatter_fusion, s32[1024]{0:T(1024)S(1)} %get-tuple-element.17, f32[1024,128]{1,0:T(8,128)S(1)} %bitcast.66), kind=kCustom, calls=%fused_computation.2 | custom fusion | flops 131072 | bytes 1576960
  53.5 12.6 %multiply_bitcast_fusion = f32[8,512,128]{1,2,0:T(8,128)} fusion(f32[8,512,128]{2,1,0:T(8,128)S(1)} %bitcast.63, f32[1,8,512,512]{3,2,1,0:T(8,128)} %param.7, f32[]{:T(128)} %bitcast.61), kind=kOutput, calls=%fused_computation.7 | convolution fusion | flops 3221749760 | bytes 12582916 | tf_op jit(solution)/shard_map/sij,sjv->siv/dot_general | solution.py:27
  66.1 2.9 copy.20
  69.0 0.0 all-reduce.3.cloned.1.call-update
  69.0 0.0 all-reduce.5.cloned.1.call-start
  69.1 113.2 %all-reduce.3.cloned.1.call-done = f32[4096,128]{1,0:T(8,128)} async-done(((f32[4096,128]{1,0:T(8,128)}), f32[4096,128]{1,0:T(8,128)}) %all-reduce.3.cloned.1.call-update) | async-done | bytes 2097168 | tf_op jit(solution)/shard_map/psum | solution.py:69
  182.3 2.2 fusion.9
  184.6 0.0 all-reduce.5.cloned.1.call-update
  184.6 246.6 %all-reduce.5.cloned.1.call-done = f32[128,128]{0,1:T(8,128)} async-done(((f32[128,128]{0,1:T(8,128)}), f32[128,128]{0,1:T(8,128)}) %all-reduce.5.cloned.1.call-update) | async-done | bytes 65552 | tf_op jit(solution)/shard_map/psum | solution.py:76
  431.2 0.9 copy.22
  432.1 0.9 fusion.13
  433.0 11.7 %cholesky.16 = f32[128,128]{1,0:T(8,128)S(1)} custom-call(f32[128,128]{1,0:T(8,128)S(1)} %fusion.13), custom_call_target="Cholesky" | custom-call | tf_op jit(solution)/shard_map/jit(cholesky)/cholesky | solution.py:77
  444.8 0.6 compare_reduce_fusion
  445.4 0.7 fusion.11
  446.1 9.8 %custom-call.6 = f32[1,128,128]{1,2,0:T(8,128)S(1)} custom-call(f32[1,128,128]{2,1,0:T(8,128)S(1)} %fusion.11), custom_call_target="InvertDiagBlocksLowerTriangular" | custom-call | tf_op jit(solution)/shard_map/triangular_solve | solution.py:79
  455.9 2.0 convolution_multiply_fusion
  (10 shorter events, 0.1 us)
Async XLA Ops:
  6.5 1.6 copy-start
  6.5 175.8 %all-reduce.3.cloned.1.call-start = ((), (), s32[]{:S(2)}) async-start(), calls=%async_computation | async-start | bytes 4194304 | tf_op jit(solution)/shard_map/psum | solution.py:69
  25.9 4.7 %slice-start = ((s32[8,2,128]{2,1,0:T(2,128)}), s32[8,1,128]{2,1,0:T(1,128)S(1)}, s32[]{:S(2)}) async-start(s32[8,2,128]{2,1,0:T(2,128)} %param.8), calls=%async_computation.2 | async-start | bytes 8192 | tf_op jit(solution)/shard_map/vmap()/slice | solution.py:35
  25.9 4.7 %copy-start.2 = (s32[8,2]{0,1:T(2,128)S(1)}, s32[8,2]{0,1:T(2,128)}, u32[]{:S(2)}) copy-start(s32[8,2]{0,1:T(2,128)} %param.9) | copy-start | bytes 196
  25.9 4.7 %copy-start.3 = (s32[2]{0:T(128)S(1)}, s32[2]{0:T(128)}, u32[]{:S(2)}) copy-start(s32[2]{0:T(128)} %constant.95) | copy-start | bytes 28
  25.9 4.8 %copy-start.1 = (f32[8,2,128]{2,1,0:T(2,128)S(1)}, f32[8,2,128]{2,1,0:T(2,128)}, u32[]{:S(2)}) copy-start(f32[8,2,128]{2,1,0:T(2,128)} %param.10) | copy-start | bytes 24580
  25.9 5.6 %copy-start.4 = (s32[2]{0:T(128)S(1)}, s32[2]{0:T(128)}, u32[]{:S(2)}) copy-start(s32[2]{0:T(128)} %constant.98) | copy-start | bytes 28
  27.3 10.1 %collective-permute-start.1 = (f32[1024,128]{1,0:T(8,128)}, f32[1024,128]{1,0:T(8,128)S(1)}, u32[]{:S(2)}, u32[]{:S(2)}) collective-permute-start(f32[1024,128]{1,0:T(8,128)} %get-tuple-element.14), channel_id=1, source_target_pairs={{1,0},{2,1},{3,2},{4,3},{5,4},{6,5},{7,6},{8,7},{9,8},{10,9},{11,1... | collective-permute-start | bytes 1572872 | tf_op jit(solution)/shard_map/ppermute | solution.py:19
  30.5 7.8 %collective-permute-start = (f32[1024,128]{1,0:T(8,128)}, f32[1024,128]{1,0:T(8,128)S(1)}, u32[]{:S(2)}, u32[]{:S(2)}) collective-permute-start(f32[1024,128]{1,0:T(8,128)} %get-tuple-element.13), channel_id=1, source_target_pairs={{0,1},{1,2},{2,3},{3,4},{4,5},{5,6},{6,7},{7,8},{8,9},{9,10},{10,1... | collective-permute-start | bytes 1572872 | tf_op jit(solution)/shard_map/ppermute | solution.py:17
  69.0 362.2 %all-reduce.5.cloned.1.call-start = ((), (), s32[]{:S(2)}) async-start(), calls=%async_computation.1 | async-start | bytes 131072 | tf_op jit(solution)/shard_map/psum | solution.py:76
Sparse Core Ops, SparseCore 0:
  69.2 113.1 all-reduce.2
  187.8 243.3 all-reduce.4
where the time goes:
time: 465 us
  waiting for transfers between devices  366 us (79%)
  other arithmetic  38.4 us (8%)
  matrix products  28.8 us (6%)
  between operations  14.3 us (3%)
  local copies, waits for them, and re-layouts  14 us (3%)
    psum x1, waiting for transfers between devices, per_device(): gram_matrix = lax.psum(local_gram, ('pole', 'sub'))  247 us
    psum x1, waiting for transfers between devices, per_device(): summed_poles = lax.psum(pole_term, 'pole')  113 us
    dot_general x2, matrix products, apply_blocks(): jnp.einsum('sij,sjv->siv', blocks, fields, precision=precise, preferred_e...  23.2 us
    unnamed x5, other arithmetic  13.9 us
    another operation x3, other arithmetic, per_device(): lower_factor = jnp.linalg.cholesky(gram_matrix)  12.4 us
    another operation x2, other arithmetic, per_device(): lax.linalg.triangular_solve(lower_factor, filtered, left_side=False, lowe...  10.5 us
  transfers between devices with their start and end apart: 4, of which 4 were waited for; matrix products, arithmetic and copies ran while one was open for 0% of the time, Pallas kernels for 0%

commit v1 on v0

--- a/solution.py
+++ b/solution.py
@@ -5,6 +5,11 @@
 from jax.sharding import PartitionSpec as P
 
 precise = lax.Precision.HIGHEST
+
+
+def axis_by_axis(value, axis_one, axis_two):
+    half = lax.psum(value, axis_one)
+    return lax.psum(half, axis_two)
 
 
 def extended_2(cells, sides, width):
@@ -73,7 +78,7 @@
     local_gram = jnp.dot(
         filtered.T, filtered, precision=precise, preferred_element_type=jnp.float32
     )
-    gram_matrix = lax.psum(local_gram, ("pole", "sub"))
+    gram_matrix = axis_by_axis(local_gram, "pole", "sub")
     lower_factor = jnp.linalg.cholesky(gram_matrix)
     total_rows = sub_count * block_len * lax.axis_size("sub")
     solved = lax.linalg.triangular_solve(

time: 465 us -> 536 us (1.15)
  waiting for transfers between devices: 366 us -> 436 us
    psum x1 -> x2, waiting for transfers between devices: 247 us -> 317 us  [the longest x1 241 us: axis_by_axis(): return lax.psum(half, axis_two)]
  transfers between devices with their start and end apart: 4 -> 5, of which waited for: 4 -> 5; matrix products, arithmetic and copies ran while one was open for 0% -> 0% of each run, Pallas kernels for 0% -> 0%
where the time goes in v1:
time: 536 us; the launch traced here: 535 us
  waiting for transfers between devices  436 us (81%)
  other arithmetic  38.4 us (7%)
  matrix products  28.8 us (5%)
  local copies, waits for them, and re-layouts  14 us (3%)
  between operations  14 us (3%)
    psum x1, waiting for transfers between devices, axis_by_axis(): return lax.psum(half, axis_two)  241 us
    psum x1, waiting for transfers between devices, per_device(): summed_poles = lax.psum(pole_term, 'pole')  113 us
    psum x1, waiting for transfers between devices, axis_by_axis(): half = lax.psum(value, axis_one)  75.5 us
    dot_general x2, matrix products, apply_blocks(): jnp.einsum('sij,sjv->siv', blocks, fields, precision=precise, preferred_e...  23.2 us
    unnamed x5, other arithmetic  13.9 us
    another operation x3, other arithmetic, per_device(): lower_factor = jnp.linalg.cholesky(gram_matrix)  12.4 us
  transfers between devices with their start and end apart: 5, of which 5 were waited for; matrix products, arithmetic and copies ran while one was open for 0% of the time, Pallas kernels for 0%

profile of v1, /device:TPU:1, one launch (start us, length us, event | category | flops | bytes accessed | tf_op | source)
XLA Modules:
  0.0 534.8 jit_solution(12055273918858425361)
XLA Ops:
  6.5 0.0 copy-start
  6.5 0.0 all-reduce.4.cloned.1.call-start
  6.5 1.6 copy.38
  8.1 0.0 copy-done
  8.1 0.1 compare_and_fusion
  8.3 10.6 %fusion.2 = f32[8,512,128]{2,1,0:T(8,128)} fusion(f32[8,512,128]{2,1,0:T(8,128)S(1)} %bitcast.62, f32[1,8,512,512]{3,2,1,0:T(8,128)} %param.7), kind=kOutput, calls=%fused_computation.5 | convolution fusion | flops 3221225472 | bytes 12582912 | tf_op jit(solution)/shard_map/sij,sjv->siv/dot_general | solution.py:32
  18.8 7.0 %gather_fusion = f32[2048,128]{1,0:T(8,128)S(1)} fusion(f32[4096,128]{1,0:T(8,128)} %bitcast.64, s32[2048]{0:T(1024)S(1)} %broadcast_clamp_fusion), kind=kCustom, calls=%fused_computation | custom fusion | bytes 2105344 | tf_op jit(solution)/shard_map/jit(_take)/gather | solution.py:56
  25.9 0.0 slice-start
  25.9 0.0 copy-start.2
  25.9 0.0 copy-start.3
  25.9 0.0 copy-start.1
  25.9 0.0 copy-start.4
  25.9 0.3 broadcast_select_fusion
  26.3 1.1 fusion.27
  27.3 3.2 collective-permute-start.1
  30.5 0.0 collective-permute-start
  30.6 0.0 slice-done
  30.6 0.0 copy-done.2
  30.6 0.0 copy-done.3
  30.6 0.1 multiply_reduce_fusion
  30.7 0.0 copy-done.1
  30.7 0.1 copy.12
  31.5 0.0 copy-done.4
  31.5 0.1 and_reduce_fusion
  31.6 5.8 %collective-permute-done.1 = f32[1024,128]{1,0:T(8,128)S(1)} collective-permute-done((f32[1024,128]{1,0:T(8,128)}, f32[1024,128]{1,0:T(8,128)S(1)}, u32[]{:S(2)}, u32[]{:S(2)}) %collective-permute-start.1) | collective-permute-done | bytes 524320 | tf_op jit(solution)/shard_map/ppermute | solution.py:24
  37.4 0.7 convolution_bitcast_fusion
  38.1 0.3 collective-permute-done
  38.4 0.7 convolution_bitcast_fusion.1
  39.0 0.3 maximum_multiply_fusion
  39.4 0.1 fusion.26
  39.5 0.1 copy.16
  39.6 0.1 copy.18
  39.7 6.8 %scatter_fusion = f32[4096,128]{1,0:T(8,128)S(1)} fusion(f32[4096,128]{1,0:T(8,128)S(1)} %copy.38, s32[1024]{0:T(1024)S(1)} %get-tuple-element.18, f32[1024,128]{1,0:T(8,128)S(1)} %bitcast.67), kind=kCustom, calls=%fused_computation.1 | custom fusion | flops 131072 | bytes 1576960
  46.5 7.0 %scatter_fusion.1 = f32[4096,128]{1,0:T(8,128)S(1)} fusion(f32[4096,128]{1,0:T(8,128)S(1)} %scatter_fusion, s32[1024]{0:T(1024)S(1)} %get-tuple-element.17, f32[1024,128]{1,0:T(8,128)S(1)} %bitcast.66), kind=kCustom, calls=%fused_computation.2 | custom fusion | flops 131072 | bytes 1576960
  53.5 12.6 %multiply_bitcast_fusion = f32[8,512,128]{1,2,0:T(8,128)} fusion(f32[8,512,128]{2,1,0:T(8,128)S(1)} %bitcast.63, f32[1,8,512,512]{3,2,1,0:T(8,128)} %param.7, f32[]{:T(128)} %bitcast.61), kind=kOutput, calls=%fused_computation.7 | convolution fusion | flops 3221749760 | bytes 12582916 | tf_op jit(solution)/shard_map/sij,sjv->siv/dot_general | solution.py:32
  66.1 2.9 copy.20
  69.0 0.0 all-reduce.4.cloned.1.call-update
  69.0 0.0 all-reduce.6.cloned.1.call-start
  69.1 113.2 %all-reduce.4.cloned.1.call-done = f32[4096,128]{1,0:T(8,128)} async-done(((f32[4096,128]{1,0:T(8,128)}), f32[4096,128]{1,0:T(8,128)}) %all-reduce.4.cloned.1.call-update) | async-done | bytes 2097168 | tf_op jit(solution)/shard_map/psum | solution.py:74
  182.3 2.2 fusion.9
  184.6 0.0 all-reduce.6.cloned.1.call-update
  184.6 0.0 all-reduce.8.cloned.1.call-start
  184.6 75.5 %all-reduce.6.cloned.1.call-done = f32[128,128]{0,1:T(8,128)} async-done(((f32[128,128]{0,1:T(8,128)}), f32[128,128]{0,1:T(8,128)}) %all-reduce.6.cloned.1.call-update) | async-done | bytes 65552 | tf_op jit(solution)/shard_map/psum | solution.py:11
  260.2 0.0 all-reduce.8.cloned.1.call-update
  260.2 241.4 %all-reduce.8.cloned.1.call-done = f32[128,128]{0,1:T(8,128)} async-done(((f32[128,128]{0,1:T(8,128)}), f32[128,128]{0,1:T(8,128)}) %all-reduce.8.cloned.1.call-update) | async-done | bytes 65552 | tf_op jit(solution)/shard_map/psum | solution.py:12
  501.6 0.9 copy.22
  502.5 0.9 fusion.13
  503.4 11.7 %cholesky.16 = f32[128,128]{1,0:T(8,128)S(1)} custom-call(f32[128,128]{1,0:T(8,128)S(1)} %fusion.13), custom_call_target="Cholesky" | custom-call | tf_op jit(solution)/shard_map/jit(cholesky)/cholesky | solution.py:82
  515.1 0.6 compare_reduce_fusion
  515.8 0.7 fusion.11
  516.4 9.8 %custom-call.6 = f32[1,128,128]{1,2,0:T(8,128)S(1)} custom-call(f32[1,128,128]{2,1,0:T(8,128)S(1)} %fusion.11), custom_call_target="InvertDiagBlocksLowerTriangular" | custom-call | tf_op jit(solution)/shard_map/triangular_solve | solution.py:84
  526.3 2.0 convolution_multiply_fusion
  (10 shorter events, 0.1 us)
Async XLA Ops:
  6.5 1.6 copy-start
  6.5 175.8 %all-reduce.4.cloned.1.call-start = ((), (), s32[]{:S(2)}) async-start(), calls=%async_computation | async-start | bytes 4194304 | tf_op jit(solution)/shard_map/psum | solution.py:74
  25.9 4.7 slice-start
  25.9 4.7 copy-start.2
  25.9 4.7 copy-start.3
  25.9 4.8 copy-start.1
  25.9 5.6 %copy-start.4 = (s32[2]{0:T(128)S(1)}, s32[2]{0:T(128)}, u32[]{:S(2)}) copy-start(s32[2]{0:T(128)} %constant.98) | copy-start | bytes 28
  27.3 10.1 %collective-permute-start.1 = (f32[1024,128]{1,0:T(8,128)}, f32[1024,128]{1,0:T(8,128)S(1)}, u32[]{:S(2)}, u32[]{:S(2)}) collective-permute-start(f32[1024,128]{1,0:T(8,128)} %get-tuple-element.14), channel_id=1, source_target_pairs={{1,0},{2,1},{3,2},{4,3},{5,4},{6,5},{7,6},{8,7},{9,8},{10,9},{11,1... | collective-permute-start | bytes 1572872 | tf_op jit(solution)/shard_map/ppermute | solution.py:24
  30.5 7.8 %collective-permute-start = (f32[1024,128]{1,0:T(8,128)}, f32[1024,128]{1,0:T(8,128)S(1)}, u32[]{:S(2)}, u32[]{:S(2)}) collective-permute-start(f32[1024,128]{1,0:T(8,128)} %get-tuple-element.13), channel_id=1, source_target_pairs={{0,1},{1,2},{2,3},{3,4},{4,5},{5,6},{6,7},{7,8},{8,9},{9,10},{10,1... | collective-permute-start | bytes 1572872 | tf_op jit(solution)/shard_map/ppermute | solution.py:22
  69.0 191.1 %all-reduce.6.cloned.1.call-start = ((), (), s32[]{:S(2)}) async-start(), calls=%async_computation.1 | async-start | bytes 131072 | tf_op jit(solution)/shard_map/psum | solution.py:11
  184.6 317.0 %all-reduce.8.cloned.1.call-start = ((), (), s32[]{:S(2)}) async-start(), calls=%async_computation.2 | async-start | bytes 131072 | tf_op jit(solution)/shard_map/psum | solution.py:12
Sparse Core Ops, SparseCore 0:
  69.2 113.1 all-reduce.3
  184.9 75.2 all-reduce.5
  262.8 238.7 all-reduce.7
